TPU v7x, 32 devices: a whole 2x2x4 slice. The times are simulated.
32 devices in a mesh: gx: 4 (over x, core), gy: 4 (over z), gz: 2 (over y).
Axes of the slice: x: 2, y: 2, z: 4, core: 2. Of those that a mesh axis runs over, the one named last changes fastest.
Arguments:
- fine_coef: bfloat16 [256, 512], P(('gx', 'gy', 'gz')), may hold values from -6 to 6
- mid_leaf: bfloat16 [32, 512], P(('gx', 'gy', 'gz')), may hold values from -6 to 6
- mid_child: int32 [32, 8], P(('gx', 'gy', 'gz')), may hold values from 0 to 7, as said below
- mid_parent: int32 [32], P(('gx', 'gy', 'gz')), may hold values from 0 to 31, each once
- mid_refined: int32 [32], P(('gx', 'gy', 'gz')), may hold values 0 or 1
- fine_nbr: int32 [256, 27], P(('gx', 'gy', 'gz')), may hold values from -1 to 255, as said below
- mid_nbr: int32 [32, 27], P(('gx', 'gy', 'gz')), may hold values from -1 to 31, as said below
- coarse_nbr: int32 [4, 27], replicated, may hold values from -1 to 3, as said below
- op_factor: float32 [3, 32, 3, 8, 8], replicated, may hold values from -1 to 1
- term_weight: float32 [32], replicated, may hold values from 0.05 to 1
Outputs:
- fine_out: float32 [256, 512], P(('gx', 'gy', 'gz'))
- mid_out: float32 [32, 512], P(('gx', 'gy', 'gz'))
Inputs may be any that keep to these rules, and one draw needn't show every extreme that they name: `fine_nbr`: column d names the fine box adjacent across displacement (d // 9 - 1, d // 3 % 3 - 1, d % 3 - 1), or -1. Column 13 is the row's own box. Box g lies on device g // 8; the named box's device differs from the row's device along each of gx, gy, gz by 0 or by that component of the displacement. `mid_nbr`: column d names the middle box adjacent across displacement (d // 9 - 1, d // 3 % 3 - 1, d % 3 - 1), or -1. Column 13 is the row's own box. Box g lies on device g; the named box's device differs from the row's device along each of gx, gy, gz by 0 or by that component of the displacement. `coarse_nbr`: column d names the coarse box adjacent across displacement (d // 9 - 1, d // 3 % 3 - 1, d % 3 - 1), or -1. Column 13 is the row's own box. `mid_child`: the 1 row of one device together name each of its 8 local fine slots exactly once. `mid_parent`: each value appears once.
All inputs are finite; a program needn't handle non-finite values. No bound on the sum of `mid_refined` on one device may be relied on, other than what follows from the above.
Results may differ from a plain program's by a relative error of at most 0.006.
Values may be sent and summed in bfloat16 or wider, within the bound.
A program may use at most 64 MiB of HBM per device.

v0:
```python
import math
import jax
import jax.numpy as jnp
import numpy as np
from jax import lax
from jax.sharding import PartitionSpec as P

exact_mode = lax.Precision.HIGHEST


def padded_2(cells, sides, width):
    for axis, dim in sides:
        count = lax.axis_size(axis)
        ends = count - 1
        head = lax.slice_in_dim(cells, 0, width, axis=dim)
        tail = lax.slice_in_dim(cells, cells.shape[dim] - width, cells.shape[dim], axis=dim)
        cells = jnp.concatenate(
            [
                lax.ppermute(tail, axis, [(i, (i + 1) % count) for i in range(ends)]),
                cells,
                lax.ppermute(head, axis, [((i + 1) % count, i) for i in range(ends)]),
            ],
            axis=dim,
        )
    return cells


def poly_multiply(left, right):
    result = [0.0] * (len(left) + len(right) - 1)
    for first, left_coef in enumerate(left):
        for second, right_coef in enumerate(right):
            result[first + second] += left_coef * right_coef
    return result


def poly_compose(coeffs, factor, offset):
    result = [0.0]
    power_term = [1.0]
    for coef in coeffs:
        padded = result + [0.0] * (len(power_term) - len(result))
        result = [padded[place] + coef * power_term[place] for place in range(len(power_term))]
        power_term = poly_multiply(power_term, [offset, factor])
    return result


def legendre_table(basis_order):
    polys = [[1.0], [0.0, 1.0]]
    for degree in range(1, basis_order):
        upper = [0.0] + [(2 * degree + 1) * coef for coef in polys[degree]]
        lower = [degree * coef for coef in polys[degree - 1]] + [0.0] * (
            len(upper) - len(polys[degree - 1])
        )
        polys.append([(upper[place] - lower[place]) / (degree + 1) for place in range(len(upper))])
    return [
        [math.sqrt(2 * degree + 1) * coef for coef in poly_compose(polys[degree], 2.0, -1.0)]
        for degree in range(basis_order)
    ]


def two_scale(basis_order):
    shifted = legendre_table(basis_order)
    filters = np.zeros((2, basis_order, basis_order))
    for which_half in range(2):
        for row_at in range(basis_order):
            halved = poly_compose(shifted[row_at], 0.5, 0.5 * which_half)
            for col_at in range(basis_order):
                product = poly_multiply(halved, shifted[col_at])
                total = sum((coef / (place + 1) for place, coef in enumerate(product)))
                filters[which_half, row_at, col_at] = total / math.sqrt(2.0)
    return jnp.asarray(filters, jnp.float32)


def compress(children, filters):
    box_count = children.shape[0]
    basis_order = filters.shape[1]
    cube_form = children.reshape(box_count, 2, 2, 2, basis_order, basis_order, basis_order)
    section_one = jnp.einsum("bijlxyz,ipx->bjlpyz", cube_form, filters, precision=exact_mode)
    section_two = jnp.einsum("bjlpyz,jqy->blpqz", section_one, filters, precision=exact_mode)
    section_three = jnp.einsum("blpqz,lrz->bpqr", section_two, filters, precision=exact_mode)
    return section_three.reshape(box_count, basis_order**3)


def prolong(parents, filters):
    box_count = parents.shape[0]
    basis_order = filters.shape[1]
    cube_form = parents.reshape(box_count, basis_order, basis_order, basis_order)
    section_one = jnp.einsum("bpqr,ipx->bixqr", cube_form, filters, precision=exact_mode)
    section_two = jnp.einsum("bixqr,jqy->bijxyr", section_one, filters, precision=exact_mode)
    section_three = jnp.einsum("bijxyr,lrz->bijlxyz", section_two, filters, precision=exact_mode)
    return section_three.reshape(box_count, 8, basis_order**3)


def level_tables(factors, weights):
    basis_order = factors.shape[-1]
    term_count = factors.shape[0]
    plane_size = basis_order * basis_order
    row_total = term_count * plane_size
    row_id = jnp.arange(row_total, dtype=jnp.int32)
    term_of = row_id // plane_size
    first_of = row_id // basis_order % basis_order
    second_of = row_id % basis_order
    pair_id = jnp.arange(term_count * basis_order, dtype=jnp.int32)
    select_first = ((term_of * basis_order + first_of)[:, None] == pair_id[None, :]).astype(
        jnp.float32
    )
    select_second = ((term_of * basis_order + second_of)[:, None] == pair_id[None, :]).astype(
        jnp.float32
    )
    col_id = jnp.arange(plane_size, dtype=jnp.int32)
    order_id = jnp.arange(basis_order, dtype=jnp.int32)
    spread_outer = (order_id[:, None] == (col_id // basis_order)[None, :]).astype(jnp.float32)
    spread_inner = (order_id[:, None] == (col_id % basis_order)[None, :]).astype(jnp.float32)
    across = jnp.transpose(factors, (1, 0, 3, 2)).reshape(3, term_count * basis_order, basis_order)
    left_pick = jnp.einsum("rs,esb->erb", select_first, across, precision=exact_mode)
    left_full = jnp.einsum("erb,bq->erq", left_pick, spread_outer, precision=exact_mode)
    right_pick = jnp.einsum("rs,esc->erc", select_second, across, precision=exact_mode)
    right_full = jnp.einsum("erc,cq->erq", right_pick, spread_inner, precision=exact_mode)
    weight_rows = jnp.dot(select_first, jnp.repeat(weights, basis_order), precision=exact_mode)
    blocks = weight_rows[None, None, :, None] * left_full[:, None] * right_full[None, :]
    return (factors.astype(jnp.bfloat16), blocks.astype(jnp.bfloat16))


def apply_boxes(sources, factor_bf, blocks):
    box_count = sources.shape[0]
    basis_order = factor_bf.shape[-1]
    plane_size = basis_order * basis_order
    cube_form = sources.reshape(box_count, 3, 3, 3, basis_order, plane_size)
    running = jnp.zeros((box_count * basis_order, plane_size), jnp.float32)
    for along_y in range(3):
        for along_z in range(3):
            picked = cube_form[:, :, along_y, along_z]
            mixed_terms = jnp.einsum(
                "mdax,bdxq->bamq", factor_bf, picked, preferred_element_type=jnp.float32
            ).astype(jnp.bfloat16)
            flat_terms = mixed_terms.reshape(box_count * basis_order, -1)
            running = running + jnp.dot(
                flat_terms, blocks[along_y, along_z], preferred_element_type=jnp.float32
            )
    return running.reshape(box_count, basis_order**3)


def pick_sources(source_table, near_ids):
    return source_table[jnp.maximum(near_ids, 0)] * (near_ids >= 0)[:, :, None].astype(jnp.bfloat16)


def apply_picked(source_table, near_ids, factor_bf, blocks):
    total_rows = near_ids.shape[0]
    group_rows = math.gcd(total_rows, 16)
    grouped = near_ids.reshape(total_rows // group_rows, group_rows, 27)

    def one_group(some_rows):
        return apply_boxes(pick_sources(source_table, some_rows), factor_bf, blocks)

    return lax.map(one_group, grouped).reshape(total_rows, -1)


def local_rows(near_ids, per_device):
    size_y = lax.axis_size("gy")
    size_z = lax.axis_size("gz")
    mine_x = lax.axis_index("gx")
    mine_y = lax.axis_index("gy")
    mine_z = lax.axis_index("gz")
    device = near_ids // per_device
    slot_at = near_ids % per_device
    other_x = device // (size_y * size_z)
    other_y = device // size_z % size_y
    other_z = device % size_z
    cell_at = (other_x - mine_x + 1) * 9 + (other_y - mine_y + 1) * 3 + (other_z - mine_z + 1)
    return jnp.where(near_ids >= 0, cell_at * per_device + slot_at, -1)


def near_fine(detail):
    shaped = detail.reshape((1, 1, 1) + detail.shape)
    extended = padded_2(shaped, (("gx", 0), ("gy", 1), ("gz", 2)), 1)
    return extended.reshape(-1, detail.shape[1])


def near_mid(detail):
    shaped = detail.reshape((1, 1, 1) + detail.shape)
    extended = padded_2(shaped, (("gx", 0), ("gy", 1), ("gz", 2)), 1)
    return extended.reshape(-1, detail.shape[1])


def shards(
    fine_coef,
    mid_leaf,
    mid_child,
    mid_parent,
    mid_refined,
    fine_nbr,
    mid_nbr,
    coarse_nbr,
    op_factor,
    term_weight,
):
    basis_order = op_factor.shape[-1]
    filters = two_scale(basis_order)
    mid_local = mid_child.shape[0]
    slots_dev = fine_coef.shape[0]
    coarse_count = coarse_nbr.shape[0]
    child_hot = (
        mid_child[:, :, None] == jnp.arange(slots_dev, dtype=jnp.int32)[None, None, :]
    ).astype(jnp.float32)
    refined = mid_refined.astype(jnp.float32)
    live_mask = jnp.einsum("mos,m->s", child_hot, refined, precision=exact_mode)
    children = fine_coef[mid_child].astype(jnp.float32)
    compressed = compress(children, filters)
    mid_source = jnp.where(
        mid_refined[:, None] > 0, compressed, mid_leaf.astype(jnp.float32)
    ).astype(jnp.bfloat16)
    mid_float = mid_source.astype(jnp.float32)
    spread = prolong(mid_float, filters)
    fine_from = jnp.einsum("mos,mok->sk", child_hot, spread, precision=exact_mode)
    fine_detail = (live_mask[:, None] * (fine_coef.astype(jnp.float32) - fine_from)).astype(
        jnp.bfloat16
    )
    parent = mid_parent // 8
    octant = mid_parent % 8
    octant_hot = (octant[:, None] == jnp.arange(8, dtype=jnp.int32)[None, :]).astype(jnp.float32)
    parent_hot = (parent[:, None] == jnp.arange(coarse_count, dtype=jnp.int32)[None, :]).astype(
        jnp.float32
    )
    placed = octant_hot[:, :, None] * mid_float[:, None, :]
    contribution = compress(placed, filters)
    partial_sum = jnp.dot(parent_hot.T, contribution, precision=exact_mode)
    coarse_source = lax.psum(partial_sum, ("gx", "gy", "gz"))
    fine_table = near_fine(fine_detail)
    fine_factor, fine_blocks = level_tables(op_factor[0], term_weight)
    fine_direct = apply_picked(
        fine_table, local_rows(fine_nbr, slots_dev), fine_factor, fine_blocks
    )
    parent_source = jnp.dot(parent_hot, coarse_source, precision=exact_mode)
    from_coarse = jnp.einsum(
        "mo,mok->mk", octant_hot, prolong(parent_source, filters), precision=exact_mode
    )
    mid_detail = (mid_float - from_coarse).astype(jnp.bfloat16)
    mid_table = near_mid(mid_detail)
    mid_factor, mid_blocks = level_tables(op_factor[1], term_weight)
    mid_direct = apply_picked(mid_table, local_rows(mid_nbr, mid_local), mid_factor, mid_blocks)
    coarse_table = coarse_source.astype(jnp.bfloat16)
    coarse_factor, coarse_blocks = level_tables(op_factor[2], term_weight)
    parent_out = apply_picked(coarse_table, coarse_nbr[parent], coarse_factor, coarse_blocks)
    mid_out = mid_direct + jnp.einsum(
        "mo,mok->mk", octant_hot, prolong(parent_out, filters), precision=exact_mode
    )
    fine_back = jnp.einsum(
        "mos,mok->sk", child_hot, prolong(mid_out, filters), precision=exact_mode
    )
    fine_out = live_mask[:, None] * (fine_direct + fine_back)
    return (fine_out, mid_out)


def solution(mesh):
    return jax.shard_map(
        shards,
        mesh=mesh,
        in_specs=(
            P(("gx", "gy", "gz"), None),
            P(("gx", "gy", "gz"), None),
            P(("gx", "gy", "gz"), None),
            P(("gx", "gy", "gz")),
            P(("gx", "gy", "gz")),
            P(("gx", "gy", "gz"), None),
            P(("gx", "gy", "gz"), None),
            P(),
            P(),
            P(),
        ),
        out_specs=(P(("gx", "gy", "gz"), None), P(("gx", "gy", "gz"), None)),
        check_vma=False,
    )
```

profile of v0, /device:TPU:10, one launch (start us, length us, event | category | flops | bytes accessed | tf_op | source)
XLA Modules:
  0.0 179.6 jit_solution(12119286320038687831)
XLA Ops:
  11.1 41.2 %psum.7 = f32[4,512]{1,0:T(4,128)S(1)} all-reduce(f32[4,512]{1,0:T(4,128)S(1)} %broadcast_multiply_fusion), channel_id=1, replica_groups=mesh['gx'=4,'gy'=4,'gz'=2] {'gx','gy','gz'}, use_global_device_ids=true, to_apply=%region_1.2 | all-reduce | flops 2048 | bytes 16384 | tf_op jit(solution)/shard_map/psum | solution.py:226
  54.7 2.6 %convolution_bitcast_fusion.17 = f32[1,2,2,2,8,8,8]{5,6,4,2,1,3,0:T(8,128)S(1)} fusion(f32[2,8,8,1,1,1]{2,1,5,4,3,0:T(8,128)} %constant.328, f32[2,2,8,8,8]{4,3,2,0,1:T(8,128)S(1)} %convolution_bitcast_fusion.41), kind=kOutput, calls=%fused_computation.48 | convolution fusion | flops 393216 | bytes 25088 | tf_op jit(solution)/shard_map/bijxyr,lrz->bijlxyz/dot_general | solution.py:89
  57.7 1.9 %collective-permute-start.6 = (bf16[1,1,1,1,512]{4,2,1,0,3:T(2,128)(2,1)S(1)}, bf16[1,1,1,1,512]{4,2,1,0,3:T(2,128)(2,1)S(1)}, u32[]{:S(2)}, u32[]{:S(2)}) collective-permute-start(bf16[1,1,1,1,512]{4,2,1,0,3:T(2,128)(2,1)S(1)} %fusion.60), channel_id=1, source_target_pairs={{0,8},{8,16},{16,24},{1,9},{9,17},{17,25},{2,10},{10,18},{18,26},{... | collective-permute-start | bytes 3080 | tf_op jit(solution)/shard_map/ppermute | solution.py:19
  59.6 3.6 %collective-permute-start.7 = (bf16[1,1,1,1,512]{4,2,1,0,3:T(2,128)(2,1)S(1)}, bf16[1,1,1,1,512]{4,2,1,0,3:T(2,128)(2,1)S(1)}, u32[]{:S(2)}, u32[]{:S(2)}) collective-permute-start(bf16[1,1,1,1,512]{4,2,1,0,3:T(2,128)(2,1)S(1)} %fusion.60), channel_id=1, source_target_pairs={{8,0},{16,8},{24,16},{9,1},{17,9},{25,17},{10,2},{18,10},{26,18},{... | collective-permute-start | bytes 3080 | tf_op jit(solution)/shard_map/ppermute | solution.py:21
  64.1 1.9 %convolution_bitcast_fusion.18 = f32[1,2,2,2,8,8,8]{5,6,4,2,1,3,0:T(8,128)S(1)} fusion(f32[2,8,8,1,1,1]{2,1,5,4,3,0:T(8,128)S(1)} %copy-done.6, f32[2,2,8,8,8]{4,3,2,0,1:T(8,128)S(1)} %convolution_bitcast_fusion.42), kind=kOutput, calls=%fused_computation.49 | convolution fusion | flops 393216 | bytes 25088 | tf_op jit(solution)/shard_map/bijxyr,lrz->bijlxyz/dot_general | solution.py:89
  66.5 1.9 %collective-permute-start = (bf16[1,1,1,8,512]{4,3,2,1,0:T(8,128)(2,1)S(1)}, bf16[1,1,1,8,512]{4,3,2,1,0:T(8,128)(2,1)S(1)}, u32[]{:S(2)}, u32[]{:S(2)}) collective-permute-start(bf16[1,1,1,8,512]{4,3,2,1,0:T(8,128)(2,1)S(1)} %fusion.58), channel_id=1, source_target_pairs={{0,8},{8,16},{16,24},{1,9},{9,17},{17,25},{2,10},{10,18},{18,26},{... | collective-permute-start | bytes 24584 | tf_op jit(solution)/shard_map/ppermute | solution.py:19
  68.5 3.6 %collective-permute-start.1 = (bf16[1,1,1,8,512]{4,3,2,1,0:T(8,128)(2,1)S(1)}, bf16[1,1,1,8,512]{4,3,2,1,0:T(8,128)(2,1)S(1)}, u32[]{:S(2)}, u32[]{:S(2)}) collective-permute-start(bf16[1,1,1,8,512]{4,3,2,1,0:T(8,128)(2,1)S(1)} %fusion.58), channel_id=1, source_target_pairs={{8,0},{16,8},{24,16},{9,1},{17,9},{25,17},{10,2},{18,10},{26,18},{... | collective-permute-start | bytes 24584 | tf_op jit(solution)/shard_map/ppermute | solution.py:21
  75.8 1.5 convolution_bitcast_fusion.1
  77.2 1.3 convolution_bitcast_fusion
  78.9 1.3 convolution_bitcast_fusion.3
  80.2 1.3 convolution_bitcast_fusion.2
  83.2 1.3 convolution_bitcast_fusion.4
  91.4 1.9 %convolution_bitcast_fusion.16 = f32[1,2,2,2,8,8,8]{5,6,4,2,1,3,0:T(8,128)S(1)} fusion(f32[2,8,8,1,1,1]{2,1,5,4,3,0:T(8,128)S(1)} %copy-done.6, f32[2,2,8,8,8]{4,3,2,0,1:T(8,128)S(1)} %convolution_bitcast_fusion.40), kind=kOutput, calls=%fused_computation.47 | convolution fusion | flops 393216 | bytes 25088 | tf_op jit(solution)/shard_map/bijxyr,lrz->bijlxyz/dot_general | solution.py:89
  97.1 2.0 %multiply_convert_fusion.1 = bf16[3,3,2048,64]{2,3,1,0:T(8,128)(2,1)} fusion(f32[3,2048,64]{1,2,0:T(8,128)S(1)} %fusion.155, f32[3,2048,64]{1,2,0:T(8,128)S(1)} %convolution_multiply_fusion.1), kind=kLoop, calls=%fused_computation.5 | loop fusion | flops 2359296 | bytes 5505024 | tf_op jit(solution)/shard_map/convert_element_type | solution.py:120
  99.7 3.3 %collective-permute-start.8 = (bf16[3,1,1,1,512]{4,2,1,0,3:T(2,128)(2,1)S(1)}, bf16[3,1,1,1,512]{4,2,1,0,3:T(2,128)(2,1)S(1)}, u32[]{:S(2)}, u32[]{:S(2)}) collective-permute-start(bf16[3,1,1,1,512]{4,2,1,0,3:T(2,128)(2,1)S(1)} %pad_maximum_fusion.5), channel_id=1, source_target_pairs={{0,2},{2,4},{4,6},{1,3},{3,5},{5,7},{8,10},{10,12},{12,14},{9,11},... | collective-permute-start | bytes 9224 | tf_op jit(solution)/shard_map/ppermute | solution.py:19
  103.0 2.5 %collective-permute-start.9 = (bf16[3,1,1,1,512]{4,2,1,0,3:T(2,128)(2,1)S(1)}, bf16[3,1,1,1,512]{4,2,1,0,3:T(2,128)(2,1)S(1)}, u32[]{:S(2)}, u32[]{:S(2)}) collective-permute-start(bf16[3,1,1,1,512]{4,2,1,0,3:T(2,128)(2,1)S(1)} %pad_maximum_fusion.5), channel_id=1, source_target_pairs={{2,0},{4,2},{6,4},{3,1},{5,3},{7,5},{10,8},{12,10},{14,12},{11,9},... | collective-permute-start | bytes 9224 | tf_op jit(solution)/shard_map/ppermute | solution.py:21
  106.1 2.5 %collective-permute-done.9 = bf16[3,1,1,1,512]{4,2,1,0,3:T(2,128)(2,1)S(1)} collective-permute-done((bf16[3,1,1,1,512]{4,2,1,0,3:T(2,128)(2,1)S(1)}, bf16[3,1,1,1,512]{4,2,1,0,3:T(2,128)(2,1)S(1)}, u32[]{:S(2)}, u32[]{:S(2)}) %collective-permute-start.9) | collective-permute-done | bytes 3104 | tf_op jit(solution)/shard_map/ppermute | solution.py:21
  108.6 2.5 %collective-permute-start.10 = (bf16[3,3,1,1,512]{4,2,1,0,3:T(2,128)(2,1)S(1)}, bf16[3,3,1,1,512]{4,2,1,0,3:T(2,128)(2,1)S(1)}, u32[]{:S(2)}, u32[]{:S(2)}) collective-permute-start(bf16[3,3,1,1,512]{4,2,1,0,3:T(2,128)(2,1)S(1)} %pad_maximum_fusion.4), channel_id=1, source_target_pairs={{0,1},{2,3},{4,5},{6,7},{8,9},{10,11},{12,13},{14,15},{16,17},{18,... | collective-permute-start | bytes 27656 | tf_op jit(solution)/shard_map/ppermute | solution.py:19
  111.1 1.3 collective-permute-start.11
  112.4 2.3 %collective-permute-start.2 = (bf16[3,1,1,8,512]{4,3,2,1,0:T(8,128)(2,1)S(1)}, bf16[3,1,1,8,512]{4,3,2,1,0:T(8,128)(2,1)S(1)}, u32[]{:S(2)}, u32[]{:S(2)}) collective-permute-start(bf16[3,1,1,8,512]{4,3,2,1,0:T(8,128)(2,1)S(1)} %pad_maximum_fusion.3), channel_id=1, source_target_pairs={{0,2},{2,4},{4,6},{1,3},{3,5},{5,7},{8,10},{10,12},{12,14},{9,11},... | collective-permute-start | bytes 73736 | tf_op jit(solution)/shard_map/ppermute | solution.py:19
  114.7 3.7 %collective-permute-start.3 = (bf16[3,1,1,8,512]{4,3,2,1,0:T(8,128)(2,1)S(1)}, bf16[3,1,1,8,512]{4,3,2,1,0:T(8,128)(2,1)S(1)}, u32[]{:S(2)}, u32[]{:S(2)}) collective-permute-start(bf16[3,1,1,8,512]{4,3,2,1,0:T(8,128)(2,1)S(1)} %pad_maximum_fusion.3), channel_id=1, source_target_pairs={{2,0},{4,2},{6,4},{3,1},{5,3},{7,5},{10,8},{12,10},{14,12},{11,9},... | collective-permute-start | bytes 73736 | tf_op jit(solution)/shard_map/ppermute | solution.py:21
  133.6 4.5 %collective-permute-start.4 = (bf16[3,3,1,8,512]{4,3,2,1,0:T(8,128)(2,1)S(1)}, bf16[3,3,1,8,512]{4,3,2,1,0:T(8,128)(2,1)S(1)}, u32[]{:S(2)}, u32[]{:S(2)}) collective-permute-start(bf16[3,3,1,8,512]{4,3,2,1,0:T(8,128)(2,1)S(1)} %pad_maximum_fusion.1), channel_id=1, source_target_pairs={{0,1},{2,3},{4,5},{6,7},{8,9},{10,11},{12,13},{14,15},{16,17},{18,... | collective-permute-start | bytes 221192 | tf_op jit(solution)/shard_map/ppermute | solution.py:19
  138.1 1.3 collective-permute-start.5
  139.4 1.9 %convolution_bitcast_fusion.15 = f32[1,2,2,2,8,8,8]{5,6,4,2,1,3,0:T(8,128)S(1)} fusion(f32[2,8,8,1,1,1]{2,1,5,4,3,0:T(8,128)S(1)} %copy-done.6, f32[2,2,8,8,8]{4,3,2,0,1:T(8,128)S(1)} %convolution_bitcast_fusion.39), kind=kOutput, calls=%fused_computation.46 | convolution fusion | flops 393216 | bytes 25088 | tf_op jit(solution)/shard_map/bijxyr,lrz->bijlxyz/dot_general | solution.py:89
  141.6 2.8 %collective-permute-done.5 = bf16[3,3,1,8,512]{4,3,2,1,0:T(8,128)(2,1)S(1)} collective-permute-done((bf16[3,3,1,8,512]{4,3,2,1,0:T(8,128)(2,1)S(1)}, bf16[3,3,1,8,512]{4,3,2,1,0:T(8,128)(2,1)S(1)}, u32[]{:S(2)}, u32[]{:S(2)}) %collective-permute-start.5) | collective-permute-done | bytes 73760 | tf_op jit(solution)/shard_map/ppermute | solution.py:21
  154.7 2.2 %reshape.817 = bf16[64,2048]{1,0:T(8,128)(2,1)} reshape(bf16[8,8,32,64]{3,2,1,0:T(8,128)(2,1)} %fusion.18) | data formatting | bytes 524288 | tf_op jit(solution)/shard_map/while/body/eval_jaxpr/reshape | solution.py:135
  156.9 2.2 %reshape.820 = bf16[64,2048]{1,0:T(8,128)(2,1)} reshape(bf16[8,8,32,64]{3,2,1,0:T(8,128)(2,1)} %fusion.17) | data formatting | bytes 524288 | tf_op jit(solution)/shard_map/while/body/eval_jaxpr/reshape | solution.py:135
  159.1 2.2 %reshape.821 = bf16[64,2048]{1,0:T(8,128)(2,1)} reshape(bf16[8,8,32,64]{3,2,1,0:T(8,128)(2,1)} %fusion.16) | data formatting | bytes 524288 | tf_op jit(solution)/shard_map/while/body/eval_jaxpr/reshape | solution.py:135
  161.3 2.2 %reshape.822 = bf16[64,2048]{1,0:T(8,128)(2,1)} reshape(bf16[8,8,32,64]{3,2,1,0:T(8,128)(2,1)} %fusion.15) | data formatting | bytes 524288 | tf_op jit(solution)/shard_map/while/body/eval_jaxpr/reshape | solution.py:135
  163.5 2.2 %reshape.823 = bf16[64,2048]{1,0:T(8,128)(2,1)} reshape(bf16[8,8,32,64]{3,2,1,0:T(8,128)(2,1)} %fusion.14) | data formatting | bytes 524288 | tf_op jit(solution)/shard_map/while/body/eval_jaxpr/reshape | solution.py:135
  165.7 2.2 %reshape.824 = bf16[64,2048]{1,0:T(8,128)(2,1)} reshape(bf16[8,8,32,64]{3,2,1,0:T(8,128)(2,1)} %fusion.13) | data formatting | bytes 524288 | tf_op jit(solution)/shard_map/while/body/eval_jaxpr/reshape | solution.py:135
  168.0 2.2 %reshape.825 = bf16[64,2048]{1,0:T(8,128)(2,1)} reshape(bf16[8,8,32,64]{3,2,1,0:T(8,128)(2,1)} %fusion.12) | data formatting | bytes 524288 | tf_op jit(solution)/shard_map/while/body/eval_jaxpr/reshape | solution.py:135
  (219 shorter events, 65.3 us)
Async XLA Ops:
  0.6 62.9 %copy-start.5 = (f32[2,8,8,1]{2,1,3,0:T(8,128)S(1)}, f32[2,8,8,1]{2,1,3,0:T(8,128)}, u32[]{:S(2)}) copy-start(f32[2,8,8,1]{2,1,3,0:T(8,128)} %constant.330) | copy-start | bytes 1540
  0.6 63.1 %copy-start.7 = (f32[2,8,8,1,1]{2,1,4,3,0:T(8,128)S(1)}, f32[2,8,8,1,1]{2,1,4,3,0:T(8,128)}, u32[]{:S(2)}) copy-start(f32[2,8,8,1,1]{2,1,4,3,0:T(8,128)} %constant.329) | copy-start | bytes 1540
  0.7 63.4 %copy-start.6 = (f32[2,8,8,1,1,1]{2,1,5,4,3,0:T(8,128)S(1)}, f32[2,8,8,1,1,1]{2,1,5,4,3,0:T(8,128)}, u32[]{:S(2)}) copy-start(f32[2,8,8,1,1,1]{2,1,5,4,3,0:T(8,128)} %constant.328) | copy-start | bytes 1540
  0.7 62.6 %copy-start.13 = (s32[1,8]{1,0:T(1,128)S(1)}, s32[1,8]{1,0:T(1,128)}, u32[]{:S(2)}) copy-start(s32[1,8]{1,0:T(1,128)} %param.13) | copy-start | bytes 100
  4.0 62.3 %copy-start.4 = (bf16[8,512]{1,0:T(8,128)(2,1)S(1)}, bf16[8,512]{1,0:T(8,128)(2,1)}, u32[]{:S(2)}) copy-start(bf16[8,512]{1,0:T(8,128)(2,1)} %param.11) | copy-start | bytes 24580
  4.2 68.0 %copy-start.3 = (f32[3,32,3,8,8]{1,4,3,2,0:T(8,128)S(1)}, f32[3,32,3,8,8]{1,4,3,2,0:T(8,128)}, u32[]{:S(2)}) copy-start(f32[3,32,3,8,8]{1,4,3,2,0:T(8,128)} %param.19) | copy-start | bytes 221188
  9.0 63.3 %copy-start.12 = (s32[4,27]{1,0:T(4,128)S(1)}, s32[4,27]{1,0:T(4,128)}, u32[]{:S(2)}) copy-start(s32[4,27]{1,0:T(4,128)} %param.18) | copy-start | bytes 1300
  52.4 20.6 %copy-start.10 = (s32[1,27]{1,0:T(1,128)S(1)}, s32[1,27]{1,0:T(1,128)}, u32[]{:S(2)}) copy-start(s32[1,27]{1,0:T(1,128)} %param.17) | copy-start | bytes 328
  57.7 42.0 %collective-permute-start.6 = (bf16[1,1,1,1,512]{4,2,1,0,3:T(2,128)(2,1)S(1)}, bf16[1,1,1,1,512]{4,2,1,0,3:T(2,128)(2,1)S(1)}, u32[]{:S(2)}, u32[]{:S(2)}) collective-permute-start(bf16[1,1,1,1,512]{4,2,1,0,3:T(2,128)(2,1)S(1)} %fusion.60), channel_id=1, source_target_pairs={{0,8},{8,16},{16,24},{1,9},{9,17},{17,25},{2,10},{10,18},{18,26},{... | collective-permute-start | bytes 3080 | tf_op jit(solution)/shard_map/ppermute | solution.py:19
  59.6 40.1 %collective-permute-start.7 = (bf16[1,1,1,1,512]{4,2,1,0,3:T(2,128)(2,1)S(1)}, bf16[1,1,1,1,512]{4,2,1,0,3:T(2,128)(2,1)S(1)}, u32[]{:S(2)}, u32[]{:S(2)}) collective-permute-start(bf16[1,1,1,1,512]{4,2,1,0,3:T(2,128)(2,1)S(1)} %fusion.60), channel_id=1, source_target_pairs={{8,0},{16,8},{24,16},{9,1},{17,9},{25,17},{10,2},{18,10},{26,18},{... | collective-permute-start | bytes 3080 | tf_op jit(solution)/shard_map/ppermute | solution.py:21
  66.5 45.8 %collective-permute-start = (bf16[1,1,1,8,512]{4,3,2,1,0:T(8,128)(2,1)S(1)}, bf16[1,1,1,8,512]{4,3,2,1,0:T(8,128)(2,1)S(1)}, u32[]{:S(2)}, u32[]{:S(2)}) collective-permute-start(bf16[1,1,1,8,512]{4,3,2,1,0:T(8,128)(2,1)S(1)} %fusion.58), channel_id=1, source_target_pairs={{0,8},{8,16},{16,24},{1,9},{9,17},{17,25},{2,10},{10,18},{18,26},{... | collective-permute-start | bytes 24584 | tf_op jit(solution)/shard_map/ppermute | solution.py:19
  68.5 43.9 %collective-permute-start.1 = (bf16[1,1,1,8,512]{4,3,2,1,0:T(8,128)(2,1)S(1)}, bf16[1,1,1,8,512]{4,3,2,1,0:T(8,128)(2,1)S(1)}, u32[]{:S(2)}, u32[]{:S(2)}) collective-permute-start(bf16[1,1,1,8,512]{4,3,2,1,0:T(8,128)(2,1)S(1)} %fusion.58), channel_id=1, source_target_pairs={{8,0},{16,8},{24,16},{9,1},{17,9},{25,17},{10,2},{18,10},{26,18},{... | collective-permute-start | bytes 24584 | tf_op jit(solution)/shard_map/ppermute | solution.py:21
  77.2 7.4 %copy-start.11 = (f32[32]{0:T(128)S(1)}, f32[32]{0:T(128)}, u32[]{:S(2)}) copy-start(f32[32]{0:T(128)} %param.20) | copy-start | bytes 388
  91.4 4.0 %copy-start.9 = (s32[8,27]{1,0:T(8,128)S(1)}, s32[8,27]{1,0:T(8,128)}, u32[]{:S(2)}) copy-start(s32[8,27]{1,0:T(8,128)} %param.16) | copy-start | bytes 2596
  99.7 6.3 %collective-permute-start.8 = (bf16[3,1,1,1,512]{4,2,1,0,3:T(2,128)(2,1)S(1)}, bf16[3,1,1,1,512]{4,2,1,0,3:T(2,128)(2,1)S(1)}, u32[]{:S(2)}, u32[]{:S(2)}) collective-permute-start(bf16[3,1,1,1,512]{4,2,1,0,3:T(2,128)(2,1)S(1)} %pad_maximum_fusion.5), channel_id=1, source_target_pairs={{0,2},{2,4},{4,6},{1,3},{3,5},{5,7},{8,10},{10,12},{12,14},{9,11},... | collective-permute-start | bytes 9224 | tf_op jit(solution)/shard_map/ppermute | solution.py:19
  103.0 5.5 %collective-permute-start.9 = (bf16[3,1,1,1,512]{4,2,1,0,3:T(2,128)(2,1)S(1)}, bf16[3,1,1,1,512]{4,2,1,0,3:T(2,128)(2,1)S(1)}, u32[]{:S(2)}, u32[]{:S(2)}) collective-permute-start(bf16[3,1,1,1,512]{4,2,1,0,3:T(2,128)(2,1)S(1)} %pad_maximum_fusion.5), channel_id=1, source_target_pairs={{2,0},{4,2},{6,4},{3,1},{5,3},{7,5},{10,8},{12,10},{14,12},{11,9},... | collective-permute-start | bytes 9224 | tf_op jit(solution)/shard_map/ppermute | solution.py:21
  108.6 9.9 %collective-permute-start.10 = (bf16[3,3,1,1,512]{4,2,1,0,3:T(2,128)(2,1)S(1)}, bf16[3,3,1,1,512]{4,2,1,0,3:T(2,128)(2,1)S(1)}, u32[]{:S(2)}, u32[]{:S(2)}) collective-permute-start(bf16[3,3,1,1,512]{4,2,1,0,3:T(2,128)(2,1)S(1)} %pad_maximum_fusion.4), channel_id=1, source_target_pairs={{0,1},{2,3},{4,5},{6,7},{8,9},{10,11},{12,13},{14,15},{16,17},{18,... | collective-permute-start | bytes 27656 | tf_op jit(solution)/shard_map/ppermute | solution.py:19
  111.1 7.4 %collective-permute-start.11 = (bf16[3,3,1,1,512]{4,2,1,0,3:T(2,128)(2,1)S(1)}, bf16[3,3,1,1,512]{4,2,1,0,3:T(2,128)(2,1)S(1)}, u32[]{:S(2)}, u32[]{:S(2)}) collective-permute-start(bf16[3,3,1,1,512]{4,2,1,0,3:T(2,128)(2,1)S(1)} %pad_maximum_fusion.4), channel_id=1, source_target_pairs={{1,0},{3,2},{5,4},{7,6},{9,8},{11,10},{13,12},{15,14},{17,16},{19,... | collective-permute-start | bytes 27656 | tf_op jit(solution)/shard_map/ppermute | solution.py:21
  112.4 21.1 %collective-permute-start.2 = (bf16[3,1,1,8,512]{4,3,2,1,0:T(8,128)(2,1)S(1)}, bf16[3,1,1,8,512]{4,3,2,1,0:T(8,128)(2,1)S(1)}, u32[]{:S(2)}, u32[]{:S(2)}) collective-permute-start(bf16[3,1,1,8,512]{4,3,2,1,0:T(8,128)(2,1)S(1)} %pad_maximum_fusion.3), channel_id=1, source_target_pairs={{0,2},{2,4},{4,6},{1,3},{3,5},{5,7},{8,10},{10,12},{12,14},{9,11},... | collective-permute-start | bytes 73736 | tf_op jit(solution)/shard_map/ppermute | solution.py:19
  114.7 18.8 %collective-permute-start.3 = (bf16[3,1,1,8,512]{4,3,2,1,0:T(8,128)(2,1)S(1)}, bf16[3,1,1,8,512]{4,3,2,1,0:T(8,128)(2,1)S(1)}, u32[]{:S(2)}, u32[]{:S(2)}) collective-permute-start(bf16[3,1,1,8,512]{4,3,2,1,0:T(8,128)(2,1)S(1)} %pad_maximum_fusion.3), channel_id=1, source_target_pairs={{2,0},{4,2},{6,4},{3,1},{5,3},{7,5},{10,8},{12,10},{14,12},{11,9},... | collective-permute-start | bytes 73736 | tf_op jit(solution)/shard_map/ppermute | solution.py:21
  132.8 12.9 %copy-start.8 = (f32[512]{0:T(512)}, f32[512]{0:T(512)S(1)}, u32[]{:S(2)}) copy-start(f32[512]{0:T(512)S(1)} %add.348) | copy-start | bytes 6148
  133.6 8.0 %collective-permute-start.4 = (bf16[3,3,1,8,512]{4,3,2,1,0:T(8,128)(2,1)S(1)}, bf16[3,3,1,8,512]{4,3,2,1,0:T(8,128)(2,1)S(1)}, u32[]{:S(2)}, u32[]{:S(2)}) collective-permute-start(bf16[3,3,1,8,512]{4,3,2,1,0:T(8,128)(2,1)S(1)} %pad_maximum_fusion.1), channel_id=1, source_target_pairs={{0,1},{2,3},{4,5},{6,7},{8,9},{10,11},{12,13},{14,15},{16,17},{18,... | collective-permute-start | bytes 221192 | tf_op jit(solution)/shard_map/ppermute | solution.py:19
  138.1 6.2 %collective-permute-start.5 = (bf16[3,3,1,8,512]{4,3,2,1,0:T(8,128)(2,1)S(1)}, bf16[3,3,1,8,512]{4,3,2,1,0:T(8,128)(2,1)S(1)}, u32[]{:S(2)}, u32[]{:S(2)}) collective-permute-start(bf16[3,3,1,8,512]{4,3,2,1,0:T(8,128)(2,1)S(1)} %pad_maximum_fusion.1), channel_id=1, source_target_pairs={{1,0},{3,2},{5,4},{7,6},{9,8},{11,10},{13,12},{15,14},{17,16},{19,... | collective-permute-start | bytes 221192 | tf_op jit(solution)/shard_map/ppermute | solution.py:21
  171.3 6.8 %copy-start = (bf16[64,2048]{1,0:T(8,128)(2,1)S(1)}, bf16[64,2048]{1,0:T(8,128)(2,1)}, u32[]{:S(2)}) copy-start(bf16[64,2048]{1,0:T(8,128)(2,1)} %reshape.826) | copy-start | bytes 786436
  171.8 5.9 %copy-start.2 = (bf16[64,2048]{1,0:T(8,128)(2,1)S(1)}, bf16[64,2048]{1,0:T(8,128)(2,1)}, u32[]{:S(2)}) copy-start(bf16[64,2048]{1,0:T(8,128)(2,1)} %reshape.824) | copy-start | bytes 786436
  171.8 6.2 %copy-start.1 = (bf16[64,2048]{1,0:T(8,128)(2,1)S(1)}, bf16[64,2048]{1,0:T(8,128)(2,1)}, u32[]{:S(2)}) copy-start(bf16[64,2048]{1,0:T(8,128)(2,1)} %reshape.825) | copy-start | bytes 786436
where the time goes:
time: 181 us; the launch traced here: 180 us
  matrix products  64.1 us (35%)
  blocking collectives  41.2 us (23%)
  starting transfers between devices  32.6 us (18%)
  local copies, waits for them, and re-layouts  28 us (15%)
  other arithmetic  5.35 us (3%)
  waiting for transfers between devices  5.27 us (3%)
  between operations  3.01 us (2%)
    psum x1, blocking collectives, shards(): coarse_source = lax.psum(partial_sum, ('gx', 'gy', 'gz'))  41.2 us
    reshape x27, local copies, waits for them, and re-layouts, apply_boxes(): flat_terms = mixed_terms.reshape(box_count * basis_order, -1)  19.5 us
    dot_general x27, matrix products, apply_boxes(): jnp.dot(flat_terms, blocks[along_y, along_z], preferred_element_type=jnp....  18.6 us
    ppermute x6, starting transfers between devices, padded_2(): lax.ppermute(tail, axis, [(i, (i + 1) % count) for i in range(ends)])  16.5 us
    ppermute x6, starting transfers between devices, padded_2(): lax.ppermute(head, axis, [((i + 1) % count, i) for i in range(ends)])  16.1 us
    dot_general x27, matrix products, apply_boxes(): jnp.einsum('mdax,bdxq->bamq', factor_bf, picked, preferred_element_type=j...  12.5 us
    dot_general x4, matrix products, prolong(): jnp.einsum('bijxyr,lrz->bijlxyz', section_two, filters, precision=exact_m...  8.2 us
    unnamed x6, matrix products  7.83 us
  transfers between devices with their start and end apart: 12, of which 2 were waited for; matrix products, arithmetic and copies ran while one was open for 27% of the time, Pallas kernels for 0%

commit v1 on v0

--- a/solution.py
+++ b/solution.py
@@ -223,7 +223,8 @@
     placed = octant_hot[:, :, None] * mid_float[:, None, :]
     contribution = compress(placed, filters)
     partial_sum = jnp.dot(parent_hot.T, contribution, precision=exact_mode)
-    coarse_source = lax.psum(partial_sum, ("gx", "gy", "gz"))
+    clean = jax.lax.all_gather(partial_sum, ("gx", "gy", "gz"))
+    coarse_source = jnp.sum(clean, axis=0)
     fine_table = near_fine(fine_detail)
     fine_factor, fine_blocks = level_tables(op_factor[0], term_weight)
     fine_direct = apply_picked(

time: 181 us -> 202 us (1.12)
  blocking collectives: 41.2 us -> 66 us
  matrix products: 64.1 us -> 62 us
    all_gather x0 -> x1, blocking collectives: none -> 66 us  [shards(): clean = jax.lax.all_gather(partial_sum, ('gx', 'gy', 'gz'))]
    psum x1 -> x0, blocking collectives: 41.2 us -> none  [shards(): coarse_source = lax.psum(partial_sum, ('gx', 'gy', 'gz'))]
  transfers between devices with their start and end apart: 12 -> 12, of which waited for: 2 -> 2; matrix products, arithmetic and copies ran while one was open for 27% -> 24% of each run, Pallas kernels for 0% -> 0%
where the time goes in v1:
time: 202 us; the launch traced here: 200 us
  blocking collectives  66 us (33%)
  matrix products  62 us (31%)
  starting transfers between devices  32.1 us (16%)
  local copies, waits for them, and re-layouts  28 us (14%)
  other arithmetic  5.45 us (3%)
  waiting for transfers between devices  3.62 us (2%)
  between operations  3.01 us (1%)
    all_gather x1, blocking collectives, shards(): clean = jax.lax.all_gather(partial_sum, ('gx', 'gy', 'gz'))  66 us
    reshape x27, local copies, waits for them, and re-layouts, apply_boxes(): flat_terms = mixed_terms.reshape(box_count * basis_order, -1)  19.5 us
    dot_general x27, matrix products, apply_boxes(): jnp.dot(flat_terms, blocks[along_y, along_z], preferred_element_type=jnp....  18.6 us
    ppermute x6, starting transfers between devices, padded_2(): lax.ppermute(head, axis, [((i + 1) % count, i) for i in range(ends)])  17.1 us
    ppermute x6, starting transfers between devices, padded_2(): lax.ppermute(tail, axis, [(i, (i + 1) % count) for i in range(ends)])  15 us
    dot_general x27, matrix products, apply_boxes(): jnp.einsum('mdax,bdxq->bamq', factor_bf, picked, preferred_element_type=j...  12.5 us
    unnamed x6, matrix products  7.83 us
    dot_general x4, matrix products, prolong(): jnp.einsum('bijxyr,lrz->bijlxyz', section_two, filters, precision=exact_m...  7.5 us
  transfers between devices with their start and end apart: 12, of which 2 were waited for; matrix products, arithmetic and copies ran while one was open for 24% of the time, Pallas kernels for 0%

profile of v1, /device:TPU:10, one launch (start us, length us, event | category | flops | bytes accessed | tf_op | source)
XLA Modules:
  0.0 200.1 jit_solution(10864366185902436228)
XLA Ops:
  11.0 66.0 %all-gather.1 = f32[32,4,512]{2,1,0:T(4,128)S(1)} all-gather(f32[1,4,512]{2,1,0:T(4,128)S(1)} %multiply_bitcast_fusion), channel_id=2, replica_groups=mesh['gx'=4,'gy'=4,'gz'=2] {'gx','gy','gz'}, dimensions={0}, use_global_device_ids=true | all-gather | bytes 270336 | tf_op jit(solution)/shard_map/all_gather | solution.py:226
  78.2 1.9 convolution_bitcast_fusion.17
  80.5 1.9 collective-permute-start.6
  82.4 3.6 %collective-permute-start.7 = (bf16[1,1,1,1,512]{4,2,1,0,3:T(2,128)(2,1)S(1)}, bf16[1,1,1,1,512]{4,2,1,0,3:T(2,128)(2,1)S(1)}, u32[]{:S(2)}, u32[]{:S(2)}) collective-permute-start(bf16[1,1,1,1,512]{4,2,1,0,3:T(2,128)(2,1)S(1)} %fusion.60), channel_id=1, source_target_pairs={{8,0},{16,8},{24,16},{9,1},{17,9},{25,17},{10,2},{18,10},{26,18},{... | collective-permute-start | bytes 3080 | tf_op jit(solution)/shard_map/ppermute | solution.py:21
  86.8 1.9 convolution_bitcast_fusion.18
  89.3 1.9 collective-permute-start
  91.2 3.6 %collective-permute-start.1 = (bf16[1,1,1,8,512]{4,3,2,1,0:T(8,128)(2,1)S(1)}, bf16[1,1,1,8,512]{4,3,2,1,0:T(8,128)(2,1)S(1)}, u32[]{:S(2)}, u32[]{:S(2)}) collective-permute-start(bf16[1,1,1,8,512]{4,3,2,1,0:T(8,128)(2,1)S(1)} %fusion.58), channel_id=1, source_target_pairs={{8,0},{16,8},{24,16},{9,1},{17,9},{25,17},{10,2},{18,10},{26,18},{... | collective-permute-start | bytes 24584 | tf_op jit(solution)/shard_map/ppermute | solution.py:21
  98.5 1.5 convolution_bitcast_fusion.1
  100.0 1.3 convolution_bitcast_fusion
  101.7 1.3 convolution_bitcast_fusion.3
  102.9 1.3 convolution_bitcast_fusion.2
  104.6 1.3 convolution_bitcast_fusion.5
  105.9 1.3 convolution_bitcast_fusion.4
  114.2 1.9 convolution_bitcast_fusion.16
  119.9 2.0 multiply_convert_fusion.1
  122.5 1.9 collective-permute-start.8
  124.4 4.6 %collective-permute-start.9 = (bf16[3,1,1,1,512]{4,2,1,0,3:T(2,128)(2,1)S(1)}, bf16[3,1,1,1,512]{4,2,1,0,3:T(2,128)(2,1)S(1)}, u32[]{:S(2)}, u32[]{:S(2)}) collective-permute-start(bf16[3,1,1,1,512]{4,2,1,0,3:T(2,128)(2,1)S(1)} %pad_maximum_fusion.5), channel_id=1, source_target_pairs={{2,0},{4,2},{6,4},{3,1},{5,3},{7,5},{10,8},{12,10},{14,12},{11,9},... | collective-permute-start | bytes 9224 | tf_op jit(solution)/shard_map/ppermute | solution.py:21
  130.3 1.3 collective-permute-start.10
  131.6 1.3 collective-permute-start.11
  133.0 3.4 %collective-permute-start.2 = (bf16[3,1,1,8,512]{4,3,2,1,0:T(8,128)(2,1)S(1)}, bf16[3,1,1,8,512]{4,3,2,1,0:T(8,128)(2,1)S(1)}, u32[]{:S(2)}, u32[]{:S(2)}) collective-permute-start(bf16[3,1,1,8,512]{4,3,2,1,0:T(8,128)(2,1)S(1)} %pad_maximum_fusion.3), channel_id=1, source_target_pairs={{0,2},{2,4},{4,6},{1,3},{3,5},{5,7},{8,10},{10,12},{12,14},{9,11},... | collective-permute-start | bytes 73736 | tf_op jit(solution)/shard_map/ppermute | solution.py:19
  136.4 2.7 %collective-permute-start.3 = (bf16[3,1,1,8,512]{4,3,2,1,0:T(8,128)(2,1)S(1)}, bf16[3,1,1,8,512]{4,3,2,1,0:T(8,128)(2,1)S(1)}, u32[]{:S(2)}, u32[]{:S(2)}) collective-permute-start(bf16[3,1,1,8,512]{4,3,2,1,0:T(8,128)(2,1)S(1)} %pad_maximum_fusion.3), channel_id=1, source_target_pairs={{2,0},{4,2},{6,4},{3,1},{5,3},{7,5},{10,8},{12,10},{14,12},{11,9},... | collective-permute-start | bytes 73736 | tf_op jit(solution)/shard_map/ppermute | solution.py:21
  154.2 4.5 %collective-permute-start.4 = (bf16[3,3,1,8,512]{4,3,2,1,0:T(8,128)(2,1)S(1)}, bf16[3,3,1,8,512]{4,3,2,1,0:T(8,128)(2,1)S(1)}, u32[]{:S(2)}, u32[]{:S(2)}) collective-permute-start(bf16[3,3,1,8,512]{4,3,2,1,0:T(8,128)(2,1)S(1)} %pad_maximum_fusion.1), channel_id=1, source_target_pairs={{0,1},{2,3},{4,5},{6,7},{8,9},{10,11},{12,13},{14,15},{16,17},{18,... | collective-permute-start | bytes 221192 | tf_op jit(solution)/shard_map/ppermute | solution.py:19
  158.7 1.3 collective-permute-start.5
  160.0 1.9 convolution_bitcast_fusion.15
  162.2 2.8 %collective-permute-done.5 = bf16[3,3,1,8,512]{4,3,2,1,0:T(8,128)(2,1)S(1)} collective-permute-done((bf16[3,3,1,8,512]{4,3,2,1,0:T(8,128)(2,1)S(1)}, bf16[3,3,1,8,512]{4,3,2,1,0:T(8,128)(2,1)S(1)}, u32[]{:S(2)}, u32[]{:S(2)}) %collective-permute-start.5) | collective-permute-done | bytes 73760 | tf_op jit(solution)/shard_map/ppermute | solution.py:21
  175.3 2.2 %reshape.817 = bf16[64,2048]{1,0:T(8,128)(2,1)} reshape(bf16[8,8,32,64]{3,2,1,0:T(8,128)(2,1)} %fusion.18) | data formatting | bytes 524288 | tf_op jit(solution)/shard_map/while/body/eval_jaxpr/reshape | solution.py:135
  177.5 2.2 %reshape.820 = bf16[64,2048]{1,0:T(8,128)(2,1)} reshape(bf16[8,8,32,64]{3,2,1,0:T(8,128)(2,1)} %fusion.17) | data formatting | bytes 524288 | tf_op jit(solution)/shard_map/while/body/eval_jaxpr/reshape | solution.py:135
  179.7 2.2 %reshape.821 = bf16[64,2048]{1,0:T(8,128)(2,1)} reshape(bf16[8,8,32,64]{3,2,1,0:T(8,128)(2,1)} %fusion.16) | data formatting | bytes 524288 | tf_op jit(solution)/shard_map/while/body/eval_jaxpr/reshape | solution.py:135
  181.9 2.2 %reshape.822 = bf16[64,2048]{1,0:T(8,128)(2,1)} reshape(bf16[8,8,32,64]{3,2,1,0:T(8,128)(2,1)} %fusion.15) | data formatting | bytes 524288 | tf_op jit(solution)/shard_map/while/body/eval_jaxpr/reshape | solution.py:135
  184.1 2.2 %reshape.823 = bf16[64,2048]{1,0:T(8,128)(2,1)} reshape(bf16[8,8,32,64]{3,2,1,0:T(8,128)(2,1)} %fusion.14) | data formatting | bytes 524288 | tf_op jit(solution)/shard_map/while/body/eval_jaxpr/reshape | solution.py:135
  186.3 2.2 %reshape.824 = bf16[64,2048]{1,0:T(8,128)(2,1)} reshape(bf16[8,8,32,64]{3,2,1,0:T(8,128)(2,1)} %fusion.13) | data formatting | bytes 524288 | tf_op jit(solution)/shard_map/while/body/eval_jaxpr/reshape | solution.py:135
  188.5 2.2 %reshape.825 = bf16[64,2048]{1,0:T(8,128)(2,1)} reshape(bf16[8,8,32,64]{3,2,1,0:T(8,128)(2,1)} %fusion.12) | data formatting | bytes 524288 | tf_op jit(solution)/shard_map/while/body/eval_jaxpr/reshape | solution.py:135
  (220 shorter events, 63.5 us)
Async XLA Ops:
  0.6 76.9 %copy-start.5 = (f32[2,8,8,1]{2,1,3,0:T(8,128)S(1)}, f32[2,8,8,1]{2,1,3,0:T(8,128)}, u32[]{:S(2)}) copy-start(f32[2,8,8,1]{2,1,3,0:T(8,128)} %constant.330) | copy-start | bytes 1540
  0.6 77.2 %copy-start.7 = (f32[2,8,8,1,1]{2,1,4,3,0:T(8,128)S(1)}, f32[2,8,8,1,1]{2,1,4,3,0:T(8,128)}, u32[]{:S(2)}) copy-start(f32[2,8,8,1,1]{2,1,4,3,0:T(8,128)} %constant.329) | copy-start | bytes 1540
  0.7 77.5 %copy-start.6 = (f32[2,8,8,1,1,1]{2,1,5,4,3,0:T(8,128)S(1)}, f32[2,8,8,1,1,1]{2,1,5,4,3,0:T(8,128)}, u32[]{:S(2)}) copy-start(f32[2,8,8,1,1,1]{2,1,5,4,3,0:T(8,128)} %constant.328) | copy-start | bytes 1540
  0.7 85.4 %copy-start.13 = (s32[1,8]{1,0:T(1,128)S(1)}, s32[1,8]{1,0:T(1,128)}, u32[]{:S(2)}) copy-start(s32[1,8]{1,0:T(1,128)} %param.13) | copy-start | bytes 100
  6.1 82.9 %copy-start.4 = (bf16[8,512]{1,0:T(8,128)(2,1)S(1)}, bf16[8,512]{1,0:T(8,128)(2,1)}, u32[]{:S(2)}) copy-start(bf16[8,512]{1,0:T(8,128)(2,1)} %param.11) | copy-start | bytes 24580
  7.1 87.8 %copy-start.3 = (f32[3,32,3,8,8]{1,4,3,2,0:T(8,128)S(1)}, f32[3,32,3,8,8]{1,4,3,2,0:T(8,128)}, u32[]{:S(2)}) copy-start(f32[3,32,3,8,8]{1,4,3,2,0:T(8,128)} %param.19) | copy-start | bytes 221188
  77.1 18.0 %copy-start.12 = (s32[4,27]{1,0:T(4,128)S(1)}, s32[4,27]{1,0:T(4,128)}, u32[]{:S(2)}) copy-start(s32[4,27]{1,0:T(4,128)} %param.18) | copy-start | bytes 1300
  77.2 18.5 %copy-start.10 = (s32[1,27]{1,0:T(1,128)S(1)}, s32[1,27]{1,0:T(1,128)}, u32[]{:S(2)}) copy-start(s32[1,27]{1,0:T(1,128)} %param.17) | copy-start | bytes 328
  80.5 42.0 %collective-permute-start.6 = (bf16[1,1,1,1,512]{4,2,1,0,3:T(2,128)(2,1)S(1)}, bf16[1,1,1,1,512]{4,2,1,0,3:T(2,128)(2,1)S(1)}, u32[]{:S(2)}, u32[]{:S(2)}) collective-permute-start(bf16[1,1,1,1,512]{4,2,1,0,3:T(2,128)(2,1)S(1)} %fusion.60), channel_id=1, source_target_pairs={{0,8},{8,16},{16,24},{1,9},{9,17},{17,25},{2,10},{10,18},{18,26},{... | collective-permute-start | bytes 3080 | tf_op jit(solution)/shard_map/ppermute | solution.py:19
  82.4 40.0 %collective-permute-start.7 = (bf16[1,1,1,1,512]{4,2,1,0,3:T(2,128)(2,1)S(1)}, bf16[1,1,1,1,512]{4,2,1,0,3:T(2,128)(2,1)S(1)}, u32[]{:S(2)}, u32[]{:S(2)}) collective-permute-start(bf16[1,1,1,1,512]{4,2,1,0,3:T(2,128)(2,1)S(1)} %fusion.60), channel_id=1, source_target_pairs={{8,0},{16,8},{24,16},{9,1},{17,9},{25,17},{10,2},{18,10},{26,18},{... | collective-permute-start | bytes 3080 | tf_op jit(solution)/shard_map/ppermute | solution.py:21
  89.3 43.7 %collective-permute-start = (bf16[1,1,1,8,512]{4,3,2,1,0:T(8,128)(2,1)S(1)}, bf16[1,1,1,8,512]{4,3,2,1,0:T(8,128)(2,1)S(1)}, u32[]{:S(2)}, u32[]{:S(2)}) collective-permute-start(bf16[1,1,1,8,512]{4,3,2,1,0:T(8,128)(2,1)S(1)} %fusion.58), channel_id=1, source_target_pairs={{0,8},{8,16},{16,24},{1,9},{9,17},{17,25},{2,10},{10,18},{18,26},{... | collective-permute-start | bytes 24584 | tf_op jit(solution)/shard_map/ppermute | solution.py:19
  91.2 41.8 %collective-permute-start.1 = (bf16[1,1,1,8,512]{4,3,2,1,0:T(8,128)(2,1)S(1)}, bf16[1,1,1,8,512]{4,3,2,1,0:T(8,128)(2,1)S(1)}, u32[]{:S(2)}, u32[]{:S(2)}) collective-permute-start(bf16[1,1,1,8,512]{4,3,2,1,0:T(8,128)(2,1)S(1)} %fusion.58), channel_id=1, source_target_pairs={{8,0},{16,8},{24,16},{9,1},{17,9},{25,17},{10,2},{18,10},{26,18},{... | collective-permute-start | bytes 24584 | tf_op jit(solution)/shard_map/ppermute | solution.py:21
  100.0 7.4 %copy-start.11 = (f32[32]{0:T(128)S(1)}, f32[32]{0:T(128)}, u32[]{:S(2)}) copy-start(f32[32]{0:T(128)} %param.20) | copy-start | bytes 388
  114.2 4.0 %copy-start.9 = (s32[8,27]{1,0:T(8,128)S(1)}, s32[8,27]{1,0:T(8,128)}, u32[]{:S(2)}) copy-start(s32[8,27]{1,0:T(8,128)} %param.16) | copy-start | bytes 2596
  122.5 7.0 %collective-permute-start.8 = (bf16[3,1,1,1,512]{4,2,1,0,3:T(2,128)(2,1)S(1)}, bf16[3,1,1,1,512]{4,2,1,0,3:T(2,128)(2,1)S(1)}, u32[]{:S(2)}, u32[]{:S(2)}) collective-permute-start(bf16[3,1,1,1,512]{4,2,1,0,3:T(2,128)(2,1)S(1)} %pad_maximum_fusion.5), channel_id=1, source_target_pairs={{0,2},{2,4},{4,6},{1,3},{3,5},{5,7},{8,10},{10,12},{12,14},{9,11},... | collective-permute-start | bytes 9224 | tf_op jit(solution)/shard_map/ppermute | solution.py:19
  124.4 5.9 %collective-permute-start.9 = (bf16[3,1,1,1,512]{4,2,1,0,3:T(2,128)(2,1)S(1)}, bf16[3,1,1,1,512]{4,2,1,0,3:T(2,128)(2,1)S(1)}, u32[]{:S(2)}, u32[]{:S(2)}) collective-permute-start(bf16[3,1,1,1,512]{4,2,1,0,3:T(2,128)(2,1)S(1)} %pad_maximum_fusion.5), channel_id=1, source_target_pairs={{2,0},{4,2},{6,4},{3,1},{5,3},{7,5},{10,8},{12,10},{14,12},{11,9},... | collective-permute-start | bytes 9224 | tf_op jit(solution)/shard_map/ppermute | solution.py:21
  130.3 8.7 %collective-permute-start.10 = (bf16[3,3,1,1,512]{4,2,1,0,3:T(2,128)(2,1)S(1)}, bf16[3,3,1,1,512]{4,2,1,0,3:T(2,128)(2,1)S(1)}, u32[]{:S(2)}, u32[]{:S(2)}) collective-permute-start(bf16[3,3,1,1,512]{4,2,1,0,3:T(2,128)(2,1)S(1)} %pad_maximum_fusion.4), channel_id=1, source_target_pairs={{0,1},{2,3},{4,5},{6,7},{8,9},{10,11},{12,13},{14,15},{16,17},{18,... | collective-permute-start | bytes 27656 | tf_op jit(solution)/shard_map/ppermute | solution.py:19
  131.6 7.4 %collective-permute-start.11 = (bf16[3,3,1,1,512]{4,2,1,0,3:T(2,128)(2,1)S(1)}, bf16[3,3,1,1,512]{4,2,1,0,3:T(2,128)(2,1)S(1)}, u32[]{:S(2)}, u32[]{:S(2)}) collective-permute-start(bf16[3,3,1,1,512]{4,2,1,0,3:T(2,128)(2,1)S(1)} %pad_maximum_fusion.4), channel_id=1, source_target_pairs={{1,0},{3,2},{5,4},{7,6},{9,8},{11,10},{13,12},{15,14},{17,16},{19,... | collective-permute-start | bytes 27656 | tf_op jit(solution)/shard_map/ppermute | solution.py:21
  133.0 21.1 %collective-permute-start.2 = (bf16[3,1,1,8,512]{4,3,2,1,0:T(8,128)(2,1)S(1)}, bf16[3,1,1,8,512]{4,3,2,1,0:T(8,128)(2,1)S(1)}, u32[]{:S(2)}, u32[]{:S(2)}) collective-permute-start(bf16[3,1,1,8,512]{4,3,2,1,0:T(8,128)(2,1)S(1)} %pad_maximum_fusion.3), channel_id=1, source_target_pairs={{0,2},{2,4},{4,6},{1,3},{3,5},{5,7},{8,10},{10,12},{12,14},{9,11},... | collective-permute-start | bytes 73736 | tf_op jit(solution)/shard_map/ppermute | solution.py:19
  136.4 17.8 %collective-permute-start.3 = (bf16[3,1,1,8,512]{4,3,2,1,0:T(8,128)(2,1)S(1)}, bf16[3,1,1,8,512]{4,3,2,1,0:T(8,128)(2,1)S(1)}, u32[]{:S(2)}, u32[]{:S(2)}) collective-permute-start(bf16[3,1,1,8,512]{4,3,2,1,0:T(8,128)(2,1)S(1)} %pad_maximum_fusion.3), channel_id=1, source_target_pairs={{2,0},{4,2},{6,4},{3,1},{5,3},{7,5},{10,8},{12,10},{14,12},{11,9},... | collective-permute-start | bytes 73736 | tf_op jit(solution)/shard_map/ppermute | solution.py:21
  153.4 12.9 %copy-start.8 = (f32[512]{0:T(512)}, f32[512]{0:T(512)S(1)}, u32[]{:S(2)}) copy-start(f32[512]{0:T(512)S(1)} %add.346) | copy-start | bytes 6148
  154.2 8.0 %collective-permute-start.4 = (bf16[3,3,1,8,512]{4,3,2,1,0:T(8,128)(2,1)S(1)}, bf16[3,3,1,8,512]{4,3,2,1,0:T(8,128)(2,1)S(1)}, u32[]{:S(2)}, u32[]{:S(2)}) collective-permute-start(bf16[3,3,1,8,512]{4,3,2,1,0:T(8,128)(2,1)S(1)} %pad_maximum_fusion.1), channel_id=1, source_target_pairs={{0,1},{2,3},{4,5},{6,7},{8,9},{10,11},{12,13},{14,15},{16,17},{18,... | collective-permute-start | bytes 221192 | tf_op jit(solution)/shard_map/ppermute | solution.py:19
  158.7 6.2 %collective-permute-start.5 = (bf16[3,3,1,8,512]{4,3,2,1,0:T(8,128)(2,1)S(1)}, bf16[3,3,1,8,512]{4,3,2,1,0:T(8,128)(2,1)S(1)}, u32[]{:S(2)}, u32[]{:S(2)}) collective-permute-start(bf16[3,3,1,8,512]{4,3,2,1,0:T(8,128)(2,1)S(1)} %pad_maximum_fusion.1), channel_id=1, source_target_pairs={{1,0},{3,2},{5,4},{7,6},{9,8},{11,10},{13,12},{15,14},{17,16},{19,... | collective-permute-start | bytes 221192 | tf_op jit(solution)/shard_map/ppermute | solution.py:21
  191.9 6.8 %copy-start = (bf16[64,2048]{1,0:T(8,128)(2,1)S(1)}, bf16[64,2048]{1,0:T(8,128)(2,1)}, u32[]{:S(2)}) copy-start(bf16[64,2048]{1,0:T(8,128)(2,1)} %reshape.826) | copy-start | bytes 786436
  192.4 5.9 %copy-start.2 = (bf16[64,2048]{1,0:T(8,128)(2,1)S(1)}, bf16[64,2048]{1,0:T(8,128)(2,1)}, u32[]{:S(2)}) copy-start(bf16[64,2048]{1,0:T(8,128)(2,1)} %reshape.824) | copy-start | bytes 786436
  192.4 6.2 %copy-start.1 = (bf16[64,2048]{1,0:T(8,128)(2,1)S(1)}, bf16[64,2048]{1,0:T(8,128)(2,1)}, u32[]{:S(2)}) copy-start(bf16[64,2048]{1,0:T(8,128)(2,1)} %reshape.825) | copy-start | bytes 786436
